TPU v7x, 256 devices: a whole 4x4x8 slice. The times are simulated.
256 devices in a mesh: ctx: 16 (over x, y), head: 16 (over z, core).
Axes of the slice: x: 4, y: 4, z: 8, core: 2. Of those that a mesh axis runs over, the one named last changes fastest.
Arguments:
- tokens: bfloat16 [8192, 8192], P('ctx'), may hold values from -6 to 6
- w_zx: bfloat16 [8192, 2, 8192], P('ctx', None, 'head'), may hold values from -0.0625 to 0.0625
- zx_scale: float32 [2, 8192], P(None, 'head'), may hold values from 0.5 to 2
- w_bc: bfloat16 [8192, 8, 512], P('ctx'), may hold values from -0.0625 to 0.0625
- bc_scale: float32 [8, 512], replicated, may hold values from 0.5 to 2
- w_dt: bfloat16 [8192, 128], P('ctx', 'head'), may hold values from -0.0625 to 0.0625
- conv_x: float32 [5, 8192], P(None, 'head'), may hold values from -3 to 3
- conv_bc: float32 [5, 8, 512], replicated, may hold values from -3 to 3
- tail_x: bfloat16 [3, 8192], P(None, 'head'), may hold values from -6 to 6
- tail_bc: bfloat16 [3, 8, 512], replicated, may hold values from -6 to 6
- head_params: float32 [3, 128], P(None, 'head'), may hold values from -12 to 2, as said below
- init_state: float32 [128, 64, 256], P('head'), may hold values from -1.5 to 1.5
- norm_gain: float32 [8192], P('head'), may hold values from 0.5 to 1.5
Outputs:
- mixed: bfloat16 [8192, 8192], P('ctx', 'head')
Inputs may be any that keep to these rules, and one draw needn't show every extreme that they name: `head_params`: row 0 lies in -3.5 to -2.5 and row 2 in 0.5 to 1.5.
All inputs are finite; a program needn't handle non-finite values.
Results may differ from a plain program's by a relative error of at most 0.0052.
Values may be sent and summed in bfloat16 or wider, within the bound.
A program may use at most 256 MiB of HBM per device.

v0:
```python
import jax
import jax.numpy as jnp
from jax import lax
from jax.sharding import PartitionSpec as P

H = 128
P_SIZE = 64
N = 256
G = 8
K = 4


def passed_along(x, axis, by):
    length = lax.axis_size(axis)
    pairs = [(i, i + by) for i in range(length) if 0 <= i + by < length]
    return lax.ppermute(x, axis, pairs)


def prefix(part, axis, combine, identity):
    place = lax.axis_index(axis)
    gathered = jax.tree.map(lambda a: lax.all_gather(a, axis), part)
    state = jax.tree.map(lambda a, e: jnp.zeros_like(a) + jnp.asarray(e, a.dtype), part, identity)

    def one(lap, state):
        return combine(
            state, jax.tree.map(lambda a: lax.dynamic_index_in_dim(a, lap, 0, False), gathered)
        )

    return lax.fori_loop(0, place, one, state)


def conv_silu(values, before, taps):
    length = values.shape[0]
    padded = jnp.concatenate([before, values], 0).astype(jnp.float32)
    summed = taps[K]
    for tap_index in range(K):
        summed = summed + taps[tap_index] * padded[tap_index : tap_index + length]
    return jax.nn.silu(summed).astype(jnp.bfloat16)


def pick_group(values, group_index, axis_index):
    chosen = lax.dynamic_index_in_dim(values, group_index, axis_index, keepdims=False)
    return chosen


def body(
    tokens,
    w_zx,
    zx_scale,
    w_bc,
    bc_scale,
    w_dt,
    conv_x,
    conv_bc,
    tail_x,
    tail_bc,
    head_params,
    init_state,
    norm_gain,
):
    highest = lax.Precision.HIGHEST
    tok_rows = tokens.shape[0]
    local_heads = head_params.shape[1]
    channels = local_heads * P_SIZE
    per_group = H // G
    group_index = lax.axis_index("head") * local_heads // per_group
    bc_rows = pick_group(w_bc, group_index, 1)
    bc_scales = pick_group(bc_scale, group_index, 0)
    bc_taps = pick_group(conv_bc, group_index, 1)
    bc_tail = pick_group(tail_bc, group_index, 1)
    zx_rows = w_zx.reshape(w_zx.shape[0], 2 * channels)
    pieces = (
        lax.all_gather(zx_rows, "ctx", axis=0, tiled=True),
        lax.all_gather(bc_rows, "ctx", axis=0, tiled=True),
        lax.all_gather(w_dt, "ctx", axis=0, tiled=True),
    )
    zx_sum, bc_sum, step_sum = tuple(
        (jnp.dot(tokens, piece, preferred_element_type=jnp.float32) for piece in pieces)
    )
    zx_val = (zx_sum.reshape(tok_rows, 2, channels) * zx_scale).astype(jnp.bfloat16)
    gate = zx_val[:, 0]
    inner_in = zx_val[:, 1]
    bc_val = (bc_sum * bc_scales).astype(jnp.bfloat16)
    step_size = jax.nn.softplus(step_sum + head_params[0])
    edge = jnp.concatenate([inner_in[tok_rows - (K - 1) :], bc_val[tok_rows - (K - 1) :]], 1)
    arrived = passed_along(edge, "ctx", 1)
    previous = jnp.concatenate([tail_x, bc_tail], 1)
    arrived = jnp.where(lax.axis_index("ctx") == 0, previous, arrived)
    xconv = conv_silu(inner_in, arrived[:, :channels], conv_x)
    bconv = conv_silu(bc_val, arrived[:, channels:], bc_taps)
    b_part = bconv[:, :N]
    c_part = bconv[:, N:]
    x_heads = xconv.reshape(tok_rows, local_heads, P_SIZE).astype(jnp.float32)
    rate = -jnp.exp(head_params[1]) * step_size
    cumul = jnp.cumsum(rate, 0)
    cumul_t = cumul.T
    order = jnp.arange(tok_rows)
    lower = order[:, None] >= order[None, :]
    spread = cumul_t[:, :, None] - cumul_t[:, None, :]
    decay = jnp.where(lower[None], jnp.exp(jnp.minimum(spread, 0.0)), 0.0)
    scores = jnp.dot(c_part, b_part.T, preferred_element_type=jnp.float32)
    weights = decay * scores[None] * step_size.T[:, None, :]
    inner = jnp.einsum("hts,shp->thp", weights, x_heads, precision=highest)
    log_total = cumul[tok_rows - 1]
    fade = jnp.exp(log_total[None, :] - cumul) * step_size
    local_state = jnp.einsum(
        "sh,shp,sn->hpn", fade, x_heads, b_part.astype(jnp.float32), precision=highest
    )

    def combine(earlier, later):
        return (earlier[0] + later[0], jnp.exp(later[0])[:, None, None] * earlier[1] + later[1])

    before_log, before_state = prefix(
        (log_total, local_state),
        "ctx",
        combine,
        (jnp.zeros_like(log_total), jnp.zeros_like(local_state)),
    )
    incoming = jnp.exp(before_log)[:, None, None] * init_state + before_state
    carried = (
        jnp.einsum("tn,hpn->thp", c_part.astype(jnp.float32), incoming, precision=highest)
        * jnp.exp(cumul)[:, :, None]
    )
    y_val = inner + carried + head_params[2][None, :, None] * x_heads
    gated = y_val.reshape(tok_rows, channels) * jax.nn.silu(gate.astype(jnp.float32))
    squares = jnp.sum(gated * gated, axis=1)
    slot_hits = (jnp.arange(G) == group_index).astype(jnp.float32)
    placed = slot_hits[:, None] * squares[None, :]
    group_sums = lax.psum(placed, "head")
    totals = lax.dynamic_index_in_dim(group_sums, group_index, 0, keepdims=False)
    meansq = totals / (per_group * P_SIZE)
    mixed = gated * lax.rsqrt(meansq + 1e-05)[:, None] * norm_gain
    return mixed.astype(jnp.bfloat16)


def solution(mesh):
    return jax.shard_map(
        body,
        mesh=mesh,
        in_specs=(
            P("ctx", None),
            P("ctx", None, "head"),
            P(None, "head"),
            P("ctx", None, None),
            P(),
            P("ctx", "head"),
            P(None, "head"),
            P(),
            P(None, "head"),
            P(),
            P(None, "head"),
            P("head", None, None),
            P("head"),
        ),
        out_specs=P("ctx", "head"),
        check_vma=False,
    )
```

profile of v0, /device:TPU:30, one launch (start us, length us, event | category | flops | bytes accessed | tf_op | source)
XLA Modules:
  0.0 391.0 jit_solution(2558766528780283261)
XLA Ops:
  6.5 3.3 constant_dynamic-slice_fusion.8
  10.8 2.5 copy.40
  13.5 21.8 %all_gather.20 = bf16[8192,8]{0,1:T(8,128)(2,1)S(1)} all-gather(bf16[512,8]{0,1:T(8,128)(2,1)} %param.20), channel_id=1, replica_groups=mesh['ctx'=16,'head'=16] {'ctx'}, dimensions={0}, use_global_device_ids=true | all-gather | bytes 139264 | tf_op jit(solution)/shard_map/all_gather | solution.py:75
  36.1 5.7 %convolution_add_fusion = f32[512,8]{0,1:T(8,128)S(1)} fusion(bf16[512,8192]{1,0:T(8,128)(2,1)} %param.15, bf16[8192,8]{0,1:T(8,128)(2,1)S(1)} %all_gather.20, f32[8]{0:T(128)S(1)} %get-tuple-element.93), kind=kOutput, calls=%fused_computation.30 | convolution fusion | flops 67112960 | bytes 8536096 | tf_op jit(solution)/shard_map/dot_general | solution.py:78
  45.1 42.5 %all-gather.9.cloned.1.call-done = bf16[8192,1,512]{2,0,1:T(8,128)(2,1)} async-done(((bf16[512,1,512]{2,0,1:T(8,128)(2,1)}), bf16[8192,1,512]{2,0,1:T(8,128)(2,1)}) %all-gather.9.cloned.1.call-update) | async-done | bytes 8388624 | tf_op jit(solution)/shard_map/all_gather | solution.py:74
  87.6 10.2 %fusion.27 = bf16[512,512]{1,0:T(8,128)(2,1)S(1)} fusion(bf16[512,8192]{1,0:T(8,128)(2,1)} %param.15, bf16[8192,1,512]{2,0,1:T(8,128)(2,1)} %all-gather.9.cloned.1.call-done, f32[512]{0:T(512)S(1)} %bitcast.142), kind=kOutput, calls=%fused_computation.29 | convolution fusion | flops 4295491584 | bytes 17303552 | tf_op jit(solution)/shard_map/dot_general | solution.py:78
  98.7 107.3 %all-gather.7.cloned.1.call-done = bf16[8192,1024]{1,0:T(8,128)(2,1)} async-done(((bf16[512,1024]{1,0:T(8,128)(2,1)}), bf16[8192,1024]{1,0:T(8,128)(2,1)}) %all-gather.7.cloned.1.call-update) | async-done | bytes 16777232 | tf_op jit(solution)/shard_map/all_gather | solution.py:73
  206.0 14.3 %fusion.69 = f32[512,1024]{1,0:T(8,128)S(1)} fusion(bf16[512,8192]{1,0:T(8,128)(2,1)} %param.15, bf16[8192,1024]{1,0:T(8,128)(2,1)} %all-gather.7.cloned.1.call-done), kind=kOutput, calls=%fused_computation.115 | convolution fusion | flops 8589934592 | bytes 27262976 | tf_op jit(solution)/shard_map/dot_general | solution.py:78
  220.7 1.5 collective-permute-start
  222.4 3.9 collective-permute-done
  226.5 1.5 multiply_convert_fusion.1
  228.0 2.1 copy.31
  231.5 2.5 fusion.30
  234.0 21.3 %all-gather.2 = f32[16,1,8]{2,1,0:T(1,128)S(1)} all-gather(f32[1,1,8]{2,1,0:T(1,128)S(1)} %bitcast.141), channel_id=1, replica_groups=mesh['ctx'=16,'head'=16] {'ctx'}, dimensions={0}, use_global_device_ids=true | all-gather | bytes 544 | tf_op jit(solution)/shard_map/all_gather | solution.py:21
  255.5 1.4 copy.35
  256.9 1.4 fusion.53
  258.2 8.7 %fusion.16 = f32[512,8,64]{0,2,1:T(8,128)} fusion(bf16[512,8,64]{0,2,1:T(8,128)(2,1)} %bitcast.122, f32[8,512]{1,0:T(8,128)S(1)} %get-tuple-element.83, f32[512,512]{1,0:T(8,128)S(1)} %fusion.53, f32[8,512]{1,0:T(8,128)S(1)} %add_bitcast_fusion.1, pred[512,512]{1,0:T(8,128)(4,1)S(1)} %iota_compare_fusion), kind=kOutput, calls=%fused_computation.21 | convolution fusion | flops 1621098496 | bytes 2916352 | tf_op jit(solution)/shard_map/hts,shp->thp/dot_general | solution.py:103
  266.9 44.0 %all-gather.11.cloned.1.call-done = f32[128,64,256]{2,1,0:T(8,128)} async-done(((f32[8,64,256]{2,1,0:T(8,128)}), f32[128,64,256]{2,1,0:T(8,128)}) %all-gather.11.cloned.1.call-update) | async-done | bytes 8388624 | tf_op jit(solution)/shard_map/all_gather | solution.py:21
  311.0 18.8 %while.12 = (s32[]{:T(128)}, f32[8]{0:T(128)S(1)}, f32[8,64,256]{2,1,0:T(8,128)S(1)}, s32[]{:T(128)}, f32[16,8]{1,0:T(8,128)S(1)}, /*index=5*/f32[16,8,64,256]{3,2,1,0:T(8,128)}, s32[]{:T(128)}, s32[]{:T(128)}, s32[]{:T(128)}) while((s32[]{:T(128)}, f32[8]{0:T(128)S(1)}, f32[8,64,256]{2,1,0:T(8,128)S(1)}, s32[]{:T(128)}, ...), condition=%wide.region_3.4_spmd, body=%wide.region_2.3_spmd.sunk | while | flops 262157 | bytes 1573167 | solution.py:29
  311.1 1.2 bitcast_add_fusion.3
  313.6 1.2 bitcast_add_fusion.3
  314.8 1.2 bitcast_add_fusion.3
  316.1 1.2 bitcast_add_fusion.3
  317.3 1.2 bitcast_add_fusion.3
  318.6 1.2 bitcast_add_fusion.3
  319.8 1.2 bitcast_add_fusion.3
  321.1 1.2 bitcast_add_fusion.3
  322.3 1.2 bitcast_add_fusion.3
  324.9 1.2 bitcast_add_fusion.3
  329.9 3.6 multiply_reduce_fusion
  333.5 1.6 copy.34
  335.1 48.1 %psum.7 = f32[8,512]{1,0:T(8,128)S(1)} all-reduce(f32[8,512]{1,0:T(8,128)S(1)} %broadcast_multiply_fusion), channel_id=1, replica_groups=mesh['ctx'=16,'head'=16] {'head'}, use_global_device_ids=true, to_apply=%region_5.6 | all-reduce | flops 4096 | bytes 32768 | tf_op jit(solution)/shard_map/psum | solution.py:129
  (79 shorter events, 15.9 us)
Async XLA Ops:
  6.5 6.9 %copy-start = (bf16[3,8,512]{2,1,0:T(8,128)(2,1)S(1)}, bf16[3,8,512]{2,1,0:T(8,128)(2,1)}, u32[]{:S(2)}) copy-start(bf16[3,8,512]{2,1,0:T(8,128)(2,1)} %param.24) | copy-start | bytes 73732
  6.5 38.5 %copy-start.6 = (f32[5,512]{1,0:T(8,128)S(1)}, f32[5,512]{1,0:T(8,128)}, u32[]{:S(2)}) copy-start(f32[5,512]{1,0:T(8,128)} %param.21) | copy-start | bytes 30724
  6.5 81.1 %all-gather.9.cloned.1.call-start = ((), (), s32[]{:S(2)}) async-start(), calls=%async_computation.1 | async-start | bytes 8912896 | tf_op jit(solution)/shard_map/all_gather | solution.py:74
  10.8 195.3 %all-gather.7.cloned.1.call-start = ((), (), s32[]{:S(2)}) async-start(), calls=%async_computation | async-start | bytes 17825792 | tf_op jit(solution)/shard_map/all_gather | solution.py:73
  13.4 297.6 %all-gather.11.cloned.1.call-start = ((), (), s32[]{:S(2)}) async-start(), calls=%async_computation.2 | async-start | bytes 8912896 | tf_op jit(solution)/shard_map/all_gather | solution.py:21
  97.9 0.8 copy-start.4
  98.7 121.7 %copy-start.7 = (f32[2,512]{1,0:T(2,128)S(1)}, f32[2,512]{1,0:T(2,128)}, u32[]{:S(2)}) copy-start(f32[2,512]{1,0:T(2,128)} %param.17) | copy-start | bytes 12292
  98.7 127.6 %copy-start.8 = (bf16[3,512]{1,0:T(4,128)(2,1)S(1)}, bf16[3,512]{1,0:T(4,128)(2,1)}, u32[]{:S(2)}) copy-start(bf16[3,512]{1,0:T(4,128)(2,1)} %param.23) | copy-start | bytes 9220
  206.0 20.2 %copy-start.5 = (bf16[512,512]{1,0:T(8,128)(2,1)S(1)}, bf16[512,512]{1,0:T(8,128)(2,1)}, u32[]{:S(2)}) copy-start(bf16[512,512]{1,0:T(8,128)(2,1)} %copy-done.4) | copy-start | bytes 1572868
  220.7 5.5 %collective-permute-start = (bf16[3,1024]{1,0:T(4,128)(2,1)S(1)}, bf16[3,1024]{1,0:T(4,128)(2,1)S(1)}, u32[]{:S(2)}, u32[]{:S(2)}) collective-permute-start(bf16[3,1024]{1,0:T(4,128)(2,1)S(1)} %pad_maximum_fusion), channel_id=1, source_target_pairs={{0,16},{16,32},{32,48},{48,64},{64,80},{80,96},{96,112},{112,128},... | collective-permute-start | bytes 18440 | tf_op jit(solution)/shard_map/ppermute | solution.py:16
  230.7 0.8 copy-start.1
  258.2 71.6 %copy-start.2 = (bf16[512,512]{1,0:T(8,128)(2,1)S(1)}, bf16[512,512]{1,0:T(8,128)(2,1)}, u32[]{:S(2)}) copy-start(bf16[512,512]{1,0:T(8,128)(2,1)} %copy-done.1) | copy-start | bytes 1572868
  258.2 71.6 %copy-start.3 = (bf16[512,512]{0,1:T(8,128)(2,1)S(1)}, bf16[512,512]{0,1:T(8,128)(2,1)}, u32[]{:S(2)}) copy-start(bf16[512,512]{0,1:T(8,128)(2,1)} %copy.31) | copy-start | bytes 1572868
  311.0 72.3 %copy-start.9 = (f32[512]{0:T(512)S(1)}, f32[512]{0:T(512)}, u32[]{:S(2)}) copy-start(f32[512]{0:T(512)} %param.27) | copy-start | bytes 6148
Sparse Core Ops, SparseCore 0:
  10.9 76.6 all-gather.8
  90.1 115.9 all-gather.6
  234.2 76.7 all-gather.10
where the time goes:
time: 392 us; the launch traced here: 391 us
  waiting for transfers between devices  198 us (51%)
  blocking collectives  91.2 us (23%)
  matrix products  46.4 us (12%)
  other arithmetic  24.9 us (6%)
  local copies, waits for them, and re-layouts  15.4 us (4%)
  between operations  13.4 us (3%)
    all_gather x1, waiting for transfers between devices, body(): lax.all_gather(zx_rows, 'ctx', axis=0, tiled=True)  107 us
    psum x1, blocking collectives, body(): group_sums = lax.psum(placed, 'head')  48.1 us
    all_gather x1, waiting for transfers between devices, prefix(): gathered = jax.tree.map(lambda a: lax.all_gather(a, axis), part)  44 us
    all_gather x1, waiting for transfers between devices, body(): lax.all_gather(bc_rows, 'ctx', axis=0, tiled=True)  42.5 us
    dot_general x3, matrix products, body(): jnp.dot(tokens, piece, preferred_element_type=jnp.float32)  30.3 us
    all_gather x1, blocking collectives, body(): lax.all_gather(w_dt, 'ctx', axis=0, tiled=True)  21.8 us
    all_gather x1, blocking collectives, prefix(): gathered = jax.tree.map(lambda a: lax.all_gather(a, axis), part)  21.3 us
    add x15, other arithmetic, combine(): jnp.exp(later[0])[:, None, None] * earlier[1] + later[1]  18.1 us
  transfers between devices with their start and end apart: 4, of which 4 were waited for; matrix products, arithmetic and copies ran while one was open for 9% of the time, Pallas kernels for 0%

commit v1 on v0

--- a/solution.py
+++ b/solution.py
@@ -58,6 +58,22 @@
     init_state,
     norm_gain,
 ):
+
+    def compute_block(my_data, which_axis):
+        width = lax.axis_size(which_axis)
+        ready = map(lambda p: (p, (p + 1) % width), range(width))
+        row_list = list(ready)
+        r1 = range(width)
+        prior = map(lambda p: (p, (p - 1) % width), r1)
+        found = list(prior)
+        formed, w1 = ([my_data], [my_data])
+        for _ in range(width // 2):
+            formed.append(lax.ppermute(formed[-1], axis_name=which_axis, perm=row_list))
+        for _ in range((width - 1) // 2):
+            w1.append(lax.ppermute(w1[-1], which_axis, found))
+        seen_now = jnp.concatenate([*formed[::-1], *w1[1:]], 0)
+        return jnp.roll(seen_now, (lax.axis_index(which_axis) - width // 2) * my_data.shape[0], 0)
+
     highest = lax.Precision.HIGHEST
     tok_rows = tokens.shape[0]
     local_heads = head_params.shape[1]
@@ -72,7 +88,7 @@
     pieces = (
         lax.all_gather(zx_rows, "ctx", axis=0, tiled=True),
         lax.all_gather(bc_rows, "ctx", axis=0, tiled=True),
-        lax.all_gather(w_dt, "ctx", axis=0, tiled=True),
+        compute_block(w_dt, "ctx"),
     )
     zx_sum, bc_sum, step_sum = tuple(
         (jnp.dot(tokens, piece, preferred_element_type=jnp.float32) for piece in pieces)

time: 392 us -> 393 us (level)
  starting transfers between devices: 1.56 us -> 42.6 us
  waiting for transfers between devices: 198 us -> 176 us
  blocking collectives: 91.2 us -> 69.7 us
    ppermute x0 -> x15, starting transfers between devices: none -> 41.2 us  [the longest x8 41.1 us: compute_block(): formed.append(lax.ppermute(formed[-1], axis_name=which_axis, perm=row_list))]
    all_gather x1, waiting for transfers between devices: 42.5 us -> 6.07 us  [body(): lax.all_gather(bc_rows, 'ctx', axis=0, tiled=True)]
    all_gather x1 -> x0, blocking collectives: 21.8 us -> none  [body(): lax.all_gather(w_dt, 'ctx', axis=0, tiled=True)]
    ppermute x0 -> x15, waiting for transfers between devices: none -> 14.6 us  [the longest x7 8.6 us: compute_block(): w1.append(lax.ppermute(w1[-1], which_axis, found))]
  transfers between devices with their start and end apart: 4 -> 19, of which waited for: 4 -> 18; matrix products, arithmetic and copies ran while one was open for 9% -> 9% of each run, Pallas kernels for 0% -> 0%
where the time goes in v1:
time: 393 us; the launch traced here: 391 us
  waiting for transfers between devices  176 us (45%)
  blocking collectives  69.7 us (18%)
  matrix products  46.6 us (12%)
  starting transfers between devices  42.6 us (11%)
  other arithmetic  24.9 us (6%)
  local copies, waits for them, and re-layouts  17.7 us (5%)
  between operations  13.5 us (3%)
    all_gather x1, waiting for transfers between devices, body(): lax.all_gather(zx_rows, 'ctx', axis=0, tiled=True)  107 us
    psum x1, blocking collectives, body(): group_sums = lax.psum(placed, 'head')  48.1 us
    all_gather x1, waiting for transfers between devices, prefix(): gathered = jax.tree.map(lambda a: lax.all_gather(a, axis), part)  43.8 us
    ppermute x8, starting transfers between devices, compute_block(): formed.append(lax.ppermute(formed[-1], axis_name=which_axis, perm=row_list))  41.1 us
    dot_general x3, matrix products, body(): jnp.dot(tokens, piece, preferred_element_type=jnp.float32)  30.4 us
    all_gather x1, blocking collectives, prefix(): gathered = jax.tree.map(lambda a: lax.all_gather(a, axis), part)  21.5 us
    add x15, other arithmetic, combine(): jnp.exp(later[0])[:, None, None] * earlier[1] + later[1]  18.1 us
    dot_general x1, matrix products, body(): inner = jnp.einsum('hts,shp->thp', weights, x_heads, precision=highest)  8.68 us
  transfers between devices with their start and end apart: 19, of which 18 were waited for; matrix products, arithmetic and copies ran while one was open for 9% of the time, Pallas kernels for 0%

profile of v1, /device:TPU:30, one launch (start us, length us, event | category | flops | bytes accessed | tf_op | source)
XLA Modules:
  0.0 391.3 jit_solution(8547712449785128680)
XLA Ops:
  6.5 3.3 constant_dynamic-slice_fusion.8
  10.8 2.5 copy.40
  13.4 1.9 collective-permute-start.1
  15.4 2.0 collective-permute-done.1
  17.4 5.2 %collective-permute-start.2 = (bf16[512,8]{0,1:T(8,128)(2,1)S(1)}, bf16[512,8]{0,1:T(8,128)(2,1)S(1)}, u32[]{:S(2)}, u32[]{:S(2)}) collective-permute-start(bf16[512,8]{0,1:T(8,128)(2,1)S(1)} %collective-permute-done.1), channel_id=1, source_target_pairs={{0,16},{16,32},{32,48},{48,64},{64,80},{80,96},{96,112},{112,128},... | collective-permute-start | bytes 24584 | tf_op jit(solution)/shard_map/ppermute | solution.py:71
  22.5 1.4 collective-permute-done.2
  23.9 5.6 %collective-permute-start.3 = (bf16[512,8]{0,1:T(8,128)(2,1)S(1)}, bf16[512,8]{0,1:T(8,128)(2,1)S(1)}, u32[]{:S(2)}, u32[]{:S(2)}) collective-permute-start(bf16[512,8]{0,1:T(8,128)(2,1)S(1)} %collective-permute-done.2), channel_id=1, source_target_pairs={{0,16},{16,32},{32,48},{48,64},{64,80},{80,96},{96,112},{112,128},... | collective-permute-start | bytes 24584 | tf_op jit(solution)/shard_map/ppermute | solution.py:71
  30.9 5.7 %collective-permute-start.4 = (bf16[512,8]{0,1:T(8,128)(2,1)S(1)}, bf16[512,8]{0,1:T(8,128)(2,1)S(1)}, u32[]{:S(2)}, u32[]{:S(2)}) collective-permute-start(bf16[512,8]{0,1:T(8,128)(2,1)S(1)} %collective-permute-done.3), channel_id=1, source_target_pairs={{0,16},{16,32},{32,48},{48,64},{64,80},{80,96},{96,112},{112,128},... | collective-permute-start | bytes 24584 | tf_op jit(solution)/shard_map/ppermute | solution.py:71
  38.0 5.6 %collective-permute-start.5 = (bf16[512,8]{0,1:T(8,128)(2,1)S(1)}, bf16[512,8]{0,1:T(8,128)(2,1)S(1)}, u32[]{:S(2)}, u32[]{:S(2)}) collective-permute-start(bf16[512,8]{0,1:T(8,128)(2,1)S(1)} %collective-permute-done.4), channel_id=1, source_target_pairs={{0,16},{16,32},{32,48},{48,64},{64,80},{80,96},{96,112},{112,128},... | collective-permute-start | bytes 24584 | tf_op jit(solution)/shard_map/ppermute | solution.py:71
  44.9 5.6 %collective-permute-start.6 = (bf16[512,8]{0,1:T(8,128)(2,1)S(1)}, bf16[512,8]{0,1:T(8,128)(2,1)S(1)}, u32[]{:S(2)}, u32[]{:S(2)}) collective-permute-start(bf16[512,8]{0,1:T(8,128)(2,1)S(1)} %collective-permute-done.5), channel_id=1, source_target_pairs={{0,16},{16,32},{32,48},{48,64},{64,80},{80,96},{96,112},{112,128},... | collective-permute-start | bytes 24584 | tf_op jit(solution)/shard_map/ppermute | solution.py:71
  51.9 5.7 %collective-permute-start.7 = (bf16[512,8]{0,1:T(8,128)(2,1)S(1)}, bf16[512,8]{0,1:T(8,128)(2,1)S(1)}, u32[]{:S(2)}, u32[]{:S(2)}) collective-permute-start(bf16[512,8]{0,1:T(8,128)(2,1)S(1)} %collective-permute-done.6), channel_id=1, source_target_pairs={{0,16},{16,32},{32,48},{48,64},{64,80},{80,96},{96,112},{112,128},... | collective-permute-start | bytes 24584 | tf_op jit(solution)/shard_map/ppermute | solution.py:71
  59.1 5.8 %collective-permute-start.8 = (bf16[512,8]{0,1:T(8,128)(2,1)S(1)}, bf16[512,8]{0,1:T(8,128)(2,1)S(1)}, u32[]{:S(2)}, u32[]{:S(2)}) collective-permute-start(bf16[512,8]{0,1:T(8,128)(2,1)S(1)} %collective-permute-done.7), channel_id=1, source_target_pairs={{0,16},{16,32},{32,48},{48,64},{64,80},{80,96},{96,112},{112,128},... | collective-permute-start | bytes 24584 | tf_op jit(solution)/shard_map/ppermute | solution.py:71
  67.1 6.2 %collective-permute-done.15 = bf16[512,8]{0,1:T(8,128)(2,1)S(1)} collective-permute-done((bf16[512,8]{0,1:T(8,128)(2,1)S(1)}, bf16[512,8]{0,1:T(8,128)(2,1)S(1)}, u32[]{:S(2)}, u32[]{:S(2)}) %collective-permute-start.15) | collective-permute-done | bytes 8224 | tf_op jit(solution)/shard_map/ppermute | solution.py:73
  74.2 5.8 %convolution_add_fusion = f32[8,512]{1,0:T(8,128)S(1)} fusion(bf16[512,8192]{1,0:T(8,128)(2,1)} %param.15, bf16[16384,8]{0,1:T(8,128)(2,1)S(1)} %constant_dynamic-update-slice_fusion, s32[]{:T(128)S(6)} %select_n.59, f32[8]{0:T(128)S(1)} %get-tuple-element.93), kind=kOutput, calls=%fused_computation.30 | convolution fusion | flops 67112960 | bytes 8536580 | tf_op jit(solution)/shard_map/dot_general | solution.py:94
  81.7 6.1 %all-gather.9.cloned.1.call-done = bf16[8192,1,512]{2,0,1:T(8,128)(2,1)} async-done(((bf16[512,1,512]{2,0,1:T(8,128)(2,1)}), bf16[8192,1,512]{2,0,1:T(8,128)(2,1)}) %all-gather.9.cloned.1.call-update) | async-done | bytes 8388624 | tf_op jit(solution)/shard_map/all_gather | solution.py:90
  87.8 10.2 %fusion.27 = bf16[512,512]{1,0:T(8,128)(2,1)S(1)} fusion(bf16[512,8192]{1,0:T(8,128)(2,1)} %param.15, bf16[8192,1,512]{2,0,1:T(8,128)(2,1)} %all-gather.9.cloned.1.call-done, f32[512]{0:T(512)S(1)} %bitcast.139), kind=kOutput, calls=%fused_computation.29 | convolution fusion | flops 4295491584 | bytes 17303552 | tf_op jit(solution)/shard_map/dot_general | solution.py:94
  98.9 107.4 %all-gather.7.cloned.1.call-done = bf16[8192,1024]{1,0:T(8,128)(2,1)} async-done(((bf16[512,1024]{1,0:T(8,128)(2,1)}), bf16[8192,1024]{1,0:T(8,128)(2,1)}) %all-gather.7.cloned.1.call-update) | async-done | bytes 16777232 | tf_op jit(solution)/shard_map/all_gather | solution.py:89
  206.2 14.3 %fusion.71 = f32[512,1024]{1,0:T(8,128)S(1)} fusion(bf16[512,8192]{1,0:T(8,128)(2,1)} %param.15, bf16[8192,1024]{1,0:T(8,128)(2,1)} %all-gather.7.cloned.1.call-done), kind=kOutput, calls=%fused_computation.149 | convolution fusion | flops 8589934592 | bytes 27262976 | tf_op jit(solution)/shard_map/dot_general | solution.py:94
  220.9 1.3 collective-permute-start
  222.4 4.1 %collective-permute-done = bf16[3,1024]{1,0:T(4,128)(2,1)S(1)} collective-permute-done((bf16[3,1024]{1,0:T(4,128)(2,1)S(1)}, bf16[3,1024]{1,0:T(4,128)(2,1)S(1)}, u32[]{:S(2)}, u32[]{:S(2)}) %collective-permute-start) | collective-permute-done | bytes 6176 | tf_op jit(solution)/shard_map/ppermute | solution.py:16
  226.7 1.5 multiply_convert_fusion.1
  228.2 2.1 copy.31
  231.7 2.5 fusion.30
  234.3 21.5 %all-gather.2 = f32[16,1,8]{2,1,0:T(1,128)S(1)} all-gather(f32[1,1,8]{2,1,0:T(1,128)S(1)} %bitcast.138), channel_id=1, replica_groups=mesh['ctx'=16,'head'=16] {'ctx'}, dimensions={0}, use_global_device_ids=true | all-gather | bytes 544 | tf_op jit(solution)/shard_map/all_gather | solution.py:21
  255.9 1.4 copy.35
  257.3 1.3 fusion.53
  258.7 8.7 %fusion.16 = f32[512,8,64]{0,2,1:T(8,128)} fusion(bf16[512,8,64]{0,2,1:T(8,128)(2,1)} %bitcast.119, f32[8,512]{1,0:T(8,128)S(1)} %get-tuple-element.83, f32[512,512]{1,0:T(8,128)S(1)} %fusion.53, f32[8,512]{1,0:T(8,128)S(1)} %add_bitcast_fusion.1, pred[512,512]{1,0:T(8,128)(4,1)S(1)} %iota_compare_fusion), kind=kOutput, calls=%fused_computation.21 | convolution fusion | flops 1621098496 | bytes 2916352 | tf_op jit(solution)/shard_map/hts,shp->thp/dot_general | solution.py:119
  267.4 43.8 %all-gather.11.cloned.1.call-done = f32[128,64,256]{2,1,0:T(8,128)} async-done(((f32[8,64,256]{2,1,0:T(8,128)}), f32[128,64,256]{2,1,0:T(8,128)}) %all-gather.11.cloned.1.call-update) | async-done | bytes 8388624 | tf_op jit(solution)/shard_map/all_gather | solution.py:21
  311.2 18.9 %while.12 = (s32[]{:T(128)}, f32[8]{0:T(128)S(1)}, f32[8,64,256]{2,1,0:T(8,128)S(1)}, s32[]{:T(128)}, f32[16,8]{1,0:T(8,128)S(1)}, /*index=5*/f32[16,8,64,256]{3,2,1,0:T(8,128)}, s32[]{:T(128)}, s32[]{:T(128)}, s32[]{:T(128)}) while((s32[]{:T(128)}, f32[8]{0:T(128)S(1)}, f32[8,64,256]{2,1,0:T(8,128)S(1)}, s32[]{:T(128)}, ...), condition=%wide.region_3.4_spmd, body=%wide.region_2.3_spmd.sunk | while | flops 262157 | bytes 1573167 | solution.py:29
  330.1 3.7 multiply_reduce_fusion
  333.8 1.6 copy.34
  335.4 48.1 %psum.7 = f32[8,512]{1,0:T(8,128)S(1)} all-reduce(f32[8,512]{1,0:T(8,128)S(1)} %broadcast_multiply_fusion), channel_id=1, replica_groups=mesh['ctx'=16,'head'=16] {'head'}, use_global_device_ids=true, to_apply=%region_5.6 | all-reduce | flops 4096 | bytes 32768 | tf_op jit(solution)/shard_map/psum | solution.py:145
  (140 shorter events, 35.6 us)
Async XLA Ops:
  6.5 51.1 %copy-start = (bf16[3,8,512]{2,1,0:T(8,128)(2,1)S(1)}, bf16[3,8,512]{2,1,0:T(8,128)(2,1)}, u32[]{:S(2)}) copy-start(bf16[3,8,512]{2,1,0:T(8,128)(2,1)} %param.24) | copy-start | bytes 73732
  6.5 81.3 %all-gather.9.cloned.1.call-start = ((), (), s32[]{:S(2)}) async-start(), calls=%async_computation.1 | async-start | bytes 8912896 | tf_op jit(solution)/shard_map/all_gather | solution.py:90
  10.8 195.5 %all-gather.7.cloned.1.call-start = ((), (), s32[]{:S(2)}) async-start(), calls=%async_computation | async-start | bytes 17825792 | tf_op jit(solution)/shard_map/all_gather | solution.py:89
  13.4 297.8 %all-gather.11.cloned.1.call-start = ((), (), s32[]{:S(2)}) async-start(), calls=%async_computation.2 | async-start | bytes 8912896 | tf_op jit(solution)/shard_map/all_gather | solution.py:21
  13.4 3.9 %collective-permute-start.1 = (bf16[512,8]{0,1:T(8,128)(2,1)}, bf16[512,8]{0,1:T(8,128)(2,1)S(1)}, u32[]{:S(2)}, u32[]{:S(2)}) collective-permute-start(bf16[512,8]{0,1:T(8,128)(2,1)} %param.20), channel_id=1, source_target_pairs={{0,16},{16,32},{32,48},{48,64},{64,80},{80,96},{96,112},{112,128},... | collective-permute-start | bytes 24584 | tf_op jit(solution)/shard_map/ppermute | solution.py:71
  17.4 6.5 %collective-permute-start.2 = (bf16[512,8]{0,1:T(8,128)(2,1)S(1)}, bf16[512,8]{0,1:T(8,128)(2,1)S(1)}, u32[]{:S(2)}, u32[]{:S(2)}) collective-permute-start(bf16[512,8]{0,1:T(8,128)(2,1)S(1)} %collective-permute-done.1), channel_id=1, source_target_pairs={{0,16},{16,32},{32,48},{48,64},{64,80},{80,96},{96,112},{112,128},... | collective-permute-start | bytes 24584 | tf_op jit(solution)/shard_map/ppermute | solution.py:71
  22.5 7.3 %collective-permute-start.9 = (bf16[512,8]{0,1:T(8,128)(2,1)}, bf16[512,8]{0,1:T(8,128)(2,1)S(1)}, u32[]{:S(2)}, u32[]{:S(2)}) collective-permute-start(bf16[512,8]{0,1:T(8,128)(2,1)} %param.20), channel_id=1, source_target_pairs={{0,240},{16,0},{32,16},{48,32},{64,48},{80,64},{96,80},{112,96},{1... | collective-permute-start | bytes 24584 | tf_op jit(solution)/shard_map/ppermute | solution.py:73
  23.9 7.0 %collective-permute-start.3 = (bf16[512,8]{0,1:T(8,128)(2,1)S(1)}, bf16[512,8]{0,1:T(8,128)(2,1)S(1)}, u32[]{:S(2)}, u32[]{:S(2)}) collective-permute-start(bf16[512,8]{0,1:T(8,128)(2,1)S(1)} %collective-permute-done.2), channel_id=1, source_target_pairs={{0,16},{16,32},{32,48},{48,64},{64,80},{80,96},{96,112},{112,128},... | collective-permute-start | bytes 24584 | tf_op jit(solution)/shard_map/ppermute | solution.py:71
  29.8 7.7 %collective-permute-start.10 = (bf16[512,8]{0,1:T(8,128)(2,1)S(1)}, bf16[512,8]{0,1:T(8,128)(2,1)S(1)}, u32[]{:S(2)}, u32[]{:S(2)}) collective-permute-start(bf16[512,8]{0,1:T(8,128)(2,1)S(1)} %collective-permute-done.9), channel_id=1, source_target_pairs={{0,240},{16,0},{32,16},{48,32},{64,48},{80,64},{96,80},{112,96},{1... | collective-permute-start | bytes 24584 | tf_op jit(solution)/shard_map/ppermute | solution.py:73
  30.9 7.1 %collective-permute-start.4 = (bf16[512,8]{0,1:T(8,128)(2,1)S(1)}, bf16[512,8]{0,1:T(8,128)(2,1)S(1)}, u32[]{:S(2)}, u32[]{:S(2)}) collective-permute-start(bf16[512,8]{0,1:T(8,128)(2,1)S(1)} %collective-permute-done.3), channel_id=1, source_target_pairs={{0,16},{16,32},{32,48},{48,64},{64,80},{80,96},{96,112},{112,128},... | collective-permute-start | bytes 24584 | tf_op jit(solution)/shard_map/ppermute | solution.py:71
  37.5 7.0 %collective-permute-start.11 = (bf16[512,8]{0,1:T(8,128)(2,1)S(1)}, bf16[512,8]{0,1:T(8,128)(2,1)S(1)}, u32[]{:S(2)}, u32[]{:S(2)}) collective-permute-start(bf16[512,8]{0,1:T(8,128)(2,1)S(1)} %collective-permute-done.10), channel_id=1, source_target_pairs={{0,240},{16,0},{32,16},{48,32},{64,48},{80,64},{96,80},{112,96},{1... | collective-permute-start | bytes 24584 | tf_op jit(solution)/shard_map/ppermute | solution.py:73
  38.0 7.0 %collective-permute-start.5 = (bf16[512,8]{0,1:T(8,128)(2,1)S(1)}, bf16[512,8]{0,1:T(8,128)(2,1)S(1)}, u32[]{:S(2)}, u32[]{:S(2)}) collective-permute-start(bf16[512,8]{0,1:T(8,128)(2,1)S(1)} %collective-permute-done.4), channel_id=1, source_target_pairs={{0,16},{16,32},{32,48},{48,64},{64,80},{80,96},{96,112},{112,128},... | collective-permute-start | bytes 24584 | tf_op jit(solution)/shard_map/ppermute | solution.py:71
  44.6 7.0 %collective-permute-start.12 = (bf16[512,8]{0,1:T(8,128)(2,1)S(1)}, bf16[512,8]{0,1:T(8,128)(2,1)S(1)}, u32[]{:S(2)}, u32[]{:S(2)}) collective-permute-start(bf16[512,8]{0,1:T(8,128)(2,1)S(1)} %collective-permute-done.11), channel_id=1, source_target_pairs={{0,240},{16,0},{32,16},{48,32},{64,48},{80,64},{96,80},{112,96},{1... | collective-permute-start | bytes 24584 | tf_op jit(solution)/shard_map/ppermute | solution.py:73
  44.9 7.0 %collective-permute-start.6 = (bf16[512,8]{0,1:T(8,128)(2,1)S(1)}, bf16[512,8]{0,1:T(8,128)(2,1)S(1)}, u32[]{:S(2)}, u32[]{:S(2)}) collective-permute-start(bf16[512,8]{0,1:T(8,128)(2,1)S(1)} %collective-permute-done.5), channel_id=1, source_target_pairs={{0,16},{16,32},{32,48},{48,64},{64,80},{80,96},{96,112},{112,128},... | collective-permute-start | bytes 24584 | tf_op jit(solution)/shard_map/ppermute | solution.py:71
  51.5 7.3 %collective-permute-start.13 = (bf16[512,8]{0,1:T(8,128)(2,1)S(1)}, bf16[512,8]{0,1:T(8,128)(2,1)S(1)}, u32[]{:S(2)}, u32[]{:S(2)}) collective-permute-start(bf16[512,8]{0,1:T(8,128)(2,1)S(1)} %collective-permute-done.12), channel_id=1, source_target_pairs={{0,240},{16,0},{32,16},{48,32},{64,48},{80,64},{96,80},{112,96},{1... | collective-permute-start | bytes 24584 | tf_op jit(solution)/shard_map/ppermute | solution.py:73
  51.9 7.2 %collective-permute-start.7 = (bf16[512,8]{0,1:T(8,128)(2,1)S(1)}, bf16[512,8]{0,1:T(8,128)(2,1)S(1)}, u32[]{:S(2)}, u32[]{:S(2)}) collective-permute-start(bf16[512,8]{0,1:T(8,128)(2,1)S(1)} %collective-permute-done.6), channel_id=1, source_target_pairs={{0,16},{16,32},{32,48},{48,64},{64,80},{80,96},{96,112},{112,128},... | collective-permute-start | bytes 24584 | tf_op jit(solution)/shard_map/ppermute | solution.py:71
  58.8 7.3 %collective-permute-start.14 = (bf16[512,8]{0,1:T(8,128)(2,1)S(1)}, bf16[512,8]{0,1:T(8,128)(2,1)S(1)}, u32[]{:S(2)}, u32[]{:S(2)}) collective-permute-start(bf16[512,8]{0,1:T(8,128)(2,1)S(1)} %collective-permute-done.13), channel_id=1, source_target_pairs={{0,240},{16,0},{32,16},{48,32},{64,48},{80,64},{96,80},{112,96},{1... | collective-permute-start | bytes 24584 | tf_op jit(solution)/shard_map/ppermute | solution.py:73
  59.1 7.3 %collective-permute-start.8 = (bf16[512,8]{0,1:T(8,128)(2,1)S(1)}, bf16[512,8]{0,1:T(8,128)(2,1)S(1)}, u32[]{:S(2)}, u32[]{:S(2)}) collective-permute-start(bf16[512,8]{0,1:T(8,128)(2,1)S(1)} %collective-permute-done.7), channel_id=1, source_target_pairs={{0,16},{16,32},{32,48},{48,64},{64,80},{80,96},{96,112},{112,128},... | collective-permute-start | bytes 24584 | tf_op jit(solution)/shard_map/ppermute | solution.py:71
  66.1 7.3 %collective-permute-start.15 = (bf16[512,8]{0,1:T(8,128)(2,1)S(1)}, bf16[512,8]{0,1:T(8,128)(2,1)S(1)}, u32[]{:S(2)}, u32[]{:S(2)}) collective-permute-start(bf16[512,8]{0,1:T(8,128)(2,1)S(1)} %collective-permute-done.14), channel_id=1, source_target_pairs={{0,240},{16,0},{32,16},{48,32},{64,48},{80,64},{96,80},{112,96},{1... | collective-permute-start | bytes 24584 | tf_op jit(solution)/shard_map/ppermute | solution.py:73
  98.1 0.8 copy-start.5
  98.9 121.7 %copy-start.7 = (f32[2,512]{1,0:T(2,128)S(1)}, f32[2,512]{1,0:T(2,128)}, u32[]{:S(2)}) copy-start(f32[2,512]{1,0:T(2,128)} %param.17) | copy-start | bytes 12292
  98.9 127.6 %copy-start.8 = (bf16[3,512]{1,0:T(4,128)(2,1)S(1)}, bf16[3,512]{1,0:T(4,128)(2,1)}, u32[]{:S(2)}) copy-start(bf16[3,512]{1,0:T(4,128)(2,1)} %param.23) | copy-start | bytes 9220
  206.2 20.2 %copy-start.6 = (bf16[512,512]{1,0:T(8,128)(2,1)S(1)}, bf16[512,512]{1,0:T(8,128)(2,1)}, u32[]{:S(2)}) copy-start(bf16[512,512]{1,0:T(8,128)(2,1)} %copy-done.5) | copy-start | bytes 1572868
  220.9 5.5 %collective-permute-start = (bf16[3,1024]{1,0:T(4,128)(2,1)S(1)}, bf16[3,1024]{1,0:T(4,128)(2,1)S(1)}, u32[]{:S(2)}, u32[]{:S(2)}) collective-permute-start(bf16[3,1024]{1,0:T(4,128)(2,1)S(1)} %pad_maximum_fusion), channel_id=1, source_target_pairs={{0,16},{16,32},{32,48},{48,64},{64,80},{80,96},{96,112},{112,128},... | collective-permute-start | bytes 18440 | tf_op jit(solution)/shard_map/ppermute | solution.py:16
  230.9 0.8 copy-start.2
  258.7 71.4 %copy-start.3 = (bf16[512,512]{1,0:T(8,128)(2,1)S(1)}, bf16[512,512]{1,0:T(8,128)(2,1)}, u32[]{:S(2)}) copy-start(bf16[512,512]{1,0:T(8,128)(2,1)} %copy-done.2) | copy-start | bytes 1572868
  258.7 71.4 %copy-start.4 = (bf16[512,512]{0,1:T(8,128)(2,1)S(1)}, bf16[512,512]{0,1:T(8,128)(2,1)}, u32[]{:S(2)}) copy-start(bf16[512,512]{0,1:T(8,128)(2,1)} %copy.31) | copy-start | bytes 1572868
  311.2 73.6 %copy-start.1 = (bf16[3,8,512]{2,1,0:T(8,128)(2,1)S(1)}, bf16[3,8,512]{2,1,0:T(8,128)(2,1)}, u32[]{:S(2)}) copy-start(bf16[3,8,512]{2,1,0:T(8,128)(2,1)} %param.24) | copy-start | bytes 73732
  311.2 72.4 %copy-start.9 = (f32[512]{0:T(512)S(1)}, f32[512]{0:T(512)}, u32[]{:S(2)}) copy-start(f32[512]{0:T(512)} %param.27) | copy-start | bytes 6148
Sparse Core Ops, SparseCore 0:
  10.9 76.8 all-gather.8
  90.2 115.9 all-gather.6
  234.3 76.7 all-gather.10
